TPU v7x, 256 devices: a whole 4x4x8 slice. The times are simulated.
256 devices in a mesh: gx: 16 (over x, y_lo, core), gy: 16 (over y_hi, z).
Axes of the slice: x: 4, y: 4 (y_hi: 2, y_lo: 2; y = y_hi * 2 + y_lo), z: 8, core: 2. Of those that a mesh axis runs over, the one named last changes fastest.
Arguments:
- object_field: float32 [2, 1024, 1024], P(None, 'gy', 'gx'), may hold values from -1 to 1
- probe_modes: float32 [2, 1024, 128], P(None, ('gy', 'gx')), may hold values from -1.5 to 1.5
- positions: int32 [16, 16, 12, 2], P('gy', 'gx'), may hold values from 4 to 60, as said below
- amplitudes: float32 [16, 16, 12, 128, 128], P('gy', 'gx'), may hold values from 0 to 2
Outputs:
- object_out: float32 [2, 1024, 1024], P(None, 'gy', 'gx')
- probe_out: float32 [2, 1024, 128], P(None, ('gy', 'gx'))
Inputs may be any that keep to these rules, and one draw needn't show every extreme that they name: `positions`: each entry is a (row, column) inside its own tile; the centres of one tile lie at distinct cells of the 16 grid, each moved from the cell's middle by at most 4 cells along each dimension.
All inputs are finite; a program needn't handle non-finite values.
Results may differ from a plain program's by a relative error of at most 0.00065.
The roundings to bfloat16 on the way count: a program that leaves them out, or rounds other values in their place, can miss the bound.
Values sent between devices are 32-bit elements; how exact they have to be, the bound alone decides.
No kernel may reach another device: no remote copies, remote signals or barrier semaphores. Data moves between devices by JAX's collectives and lax.ppermute only.
A program may use at most 64 MiB of HBM per device.

v0:
```python
import math
import jax
import jax.numpy as jnp
from jax import lax
from jax.sharding import PartitionSpec as P

MODES = 8
ITERS = 2
SOFT_FLOOR = 0.05
OBJECT_REG = 1.0
PROBE_REG = 1.0


def from_behind(block, axis, distance):
    devices = range(lax.axis_size(axis))
    route = [(i - distance, i) for i in devices if i - distance in devices]
    return lax.ppermute(block, axis, route)


def extended_2(array, sides, width):
    for axis, dim in sides:
        peers, length = (lax.axis_size(axis), array.shape[dim])
        up = [(i, (i + 1) % peers) for i in range(peers - 1)]
        down = [(j, i) for i, j in up]
        last = lax.slice_in_dim(array, length - width, length, axis=dim)
        initial = lax.slice_in_dim(array, 0, width, axis=dim)
        before = lax.ppermute(last, axis, up)
        after = lax.ppermute(initial, axis, down)
        array = jnp.concatenate([before, array, after], axis=dim)
    return array


def tables(probe_side, sign_flip):
    indices = jnp.arange(probe_side, dtype=jnp.int32)
    phases = indices[:, None] * indices[None, :] % probe_side
    angles = phases.astype(jnp.float32) * (2.0 * math.pi / probe_side)
    factor = 1.0 / math.sqrt(probe_side)
    cosine = jnp.cos(angles) * factor
    sine_part = sign_flip * jnp.sin(angles) * factor
    left_op = jnp.stack(
        [jnp.stack([cosine, -sine_part]), jnp.stack([sine_part, cosine])]
    ).transpose(0, 2, 1, 3)
    right_op = jnp.stack(
        [jnp.stack([cosine, sine_part]), jnp.stack([-sine_part, cosine])]
    ).transpose(0, 2, 1, 3)
    return (left_op.astype(jnp.bfloat16), right_op.astype(jnp.bfloat16))


def transform(signal, operators):
    left_op, right_op = operators
    halfway = jnp.einsum(
        "dpcr,crmq->dpmq", left_op, signal, preferred_element_type=jnp.float32
    ).astype(jnp.bfloat16)
    return jnp.einsum("crmq,cqdk->drmk", halfway, right_op, preferred_element_type=jnp.float32)


def position_terms(patch_obj, probe, measured, forward, inverse):
    obj_real = patch_obj[0][:, None, :]
    obj_imag = patch_obj[1][:, None, :]
    wave_real = probe[0] * obj_real - probe[1] * obj_imag
    wave_imag = probe[0] * obj_imag + probe[1] * obj_real
    signal = jnp.stack([wave_real, wave_imag]).astype(jnp.bfloat16)
    spectrum = transform(signal, forward)
    intensity = jnp.sum(spectrum[0] * spectrum[0] + spectrum[1] * spectrum[1], axis=1)
    shrink = 1.0 - measured / jnp.sqrt(intensity + SOFT_FLOOR)
    residual = (spectrum * shrink[None, :, None, :]).astype(jnp.bfloat16)
    change = transform(residual, inverse)
    grad_real = jnp.sum(probe[0] * change[0] + probe[1] * change[1], axis=1)
    grad_imag = jnp.sum(probe[0] * change[1] - probe[1] * change[0], axis=1)
    probe_real = obj_real * change[0] + obj_imag * change[1]
    probe_imag = obj_real * change[1] - obj_imag * change[0]
    weight_probe = patch_obj[0] * patch_obj[0] + patch_obj[1] * patch_obj[1]
    return (jnp.stack([grad_real, grad_imag]), jnp.stack([probe_real, probe_imag]), weight_probe)


def fold_rows(gradient, margin, tile_side):
    extent = gradient.shape[1]
    for direction in (1, -1):
        rim_part = gradient[:, extent - margin :, :] if direction == 1 else gradient[:, :margin, :]
        offset = margin if direction == 1 else tile_side
        arrived = from_behind(rim_part, "gy", direction)
        gradient = gradient.at[:, offset : offset + margin, :].add(arrived)
    return gradient[:, margin : margin + tile_side, :]


def fold_cols(gradient, margin, tile_side):
    extent = gradient.shape[2]
    for direction in (1, -1):
        rim_part = gradient[:, :, extent - margin :] if direction == 1 else gradient[:, :, :margin]
        offset = margin if direction == 1 else tile_side
        arrived = from_behind(rim_part, "gx", direction)
        gradient = gradient.at[:, :, offset : offset + margin].add(arrived)
    return gradient[:, :, margin : margin + tile_side]


def unpack_probe(probe_rows, probe_side):
    return probe_rows.reshape(2, MODES, probe_side, probe_side).transpose(0, 2, 1, 3)


def local(object_field, probe_modes, positions, amplitudes):
    probe_side = amplitudes.shape[-1]
    margin = probe_side // 2
    tile_side = object_field.shape[1]
    centres = positions.reshape(-1, 2)
    measured_all = amplitudes.reshape(-1, probe_side, probe_side)
    forward = tables(probe_side, -1.0)
    inverse = tables(probe_side, 1.0)
    gathered = lax.all_gather(probe_modes, ("gy", "gx"), axis=1, tiled=True)
    probe = unpack_probe(gathered, probe_side)
    own_rows = probe_modes
    current = object_field
    for iteration in range(ITERS):
        extended = extended_2(current, (("gy", 1), ("gx", 2)), margin)
        weight_obj = jnp.sum(probe[0] * probe[0] + probe[1] * probe[1], axis=1)

        def visit(running, visit_item):
            grad_obj, grad_probe, weight_probe = running
            row_at, col_at, measured = visit_item
            zero_index = jnp.int32(0)
            patch_obj = lax.dynamic_slice(
                extended, (zero_index, row_at, col_at), (2, probe_side, probe_side)
            )
            g_obj, g_probe, w_probe = position_terms(patch_obj, probe, measured, forward, inverse)
            stacked = jnp.concatenate([g_obj, weight_obj[None]], axis=0)
            before = lax.dynamic_slice(
                grad_obj, (zero_index, row_at, col_at), (3, probe_side, probe_side)
            )
            grad_obj = lax.dynamic_update_slice(
                grad_obj, before + stacked, (zero_index, row_at, col_at)
            )
            return ((grad_obj, grad_probe + g_probe, weight_probe + w_probe), None)

        initial = (
            jnp.zeros((3, tile_side + probe_side, tile_side + probe_side), jnp.float32),
            jnp.zeros((2, probe_side, MODES, probe_side), jnp.float32),
            jnp.zeros((probe_side, probe_side), jnp.float32),
        )
        (grad_obj, grad_probe, weight_probe), _ = lax.scan(
            visit, initial, (centres[:, 0], centres[:, 1], measured_all)
        )
        folded = fold_cols(fold_rows(grad_obj, margin, tile_side), margin, tile_side)
        new_object = current - folded[0:2] / (folded[2] + OBJECT_REG)
        grad_rows = grad_probe.transpose(0, 2, 1, 3).reshape(2, MODES * probe_side, probe_side)
        totals, weight_total = lax.psum((grad_rows, weight_probe), ("gy", "gx"))
        whole_probe = probe.transpose(0, 2, 1, 3)
        whole_probe = whole_probe - totals.reshape(2, MODES, probe_side, probe_side) / (
            weight_total[None, None] + PROBE_REG
        )
        whole_probe = whole_probe.reshape(2, MODES * probe_side, probe_side)
        probe = unpack_probe(whole_probe, probe_side)
        row_count = own_rows.shape[1]
        own_rows = lax.dynamic_slice_in_dim(
            whole_probe, lax.axis_index(("gy", "gx")) * row_count, row_count, 1
        )
        current = new_object
    return (current, own_rows)


def solution(mesh):
    return jax.shard_map(
        local,
        mesh=mesh,
        in_specs=(
            P(None, "gy", "gx"),
            P(None, ("gy", "gx"), None),
            P("gy", "gx", None, None),
            P("gy", "gx", None, None, None),
        ),
        out_specs=(P(None, "gy", "gx"), P(None, ("gy", "gx"), None)),
        check_vma=False,
    )
```

profile of v0, /device:TPU:16, one launch (start us, length us, event | category | flops | bytes accessed | tf_op | source)
XLA Modules:
  0.0 1355.4 jit_solution(5158283582343708737)
XLA Ops:
  8.6 3.8 collective-permute-start
  12.4 5.6 collective-permute-start.1
  24.8 3.6 collective-permute-done.3
  29.3 362.2 %all-gather.2.cloned.1.call-done = f32[2,1024,128]{2,0,1:T(2,128)} async-done(((f32[2,4,128]{2,0,1:T(2,128)}), f32[2,1024,128]{2,0,1:T(2,128)}) %all-gather.2.cloned.1.call-update) | async-done | bytes 1048592 | tf_op jit(solution)/shard_map/all_gather | solution.py:108
  394.4 205.2 %while.38 = (s32[]{:T(128)}, f32[3,192,192]{2,1,0:T(8,128)}, f32[2,128,8,128]{3,1,0,2:T(8,128)}, f32[128,128]{1,0:T(8,128)}, s32[12]{0:T(128)S(1)}, /*index=5*/s...) while((s32[]{:T(128)}, f32[3,192,192]{2,1,0:T(8,128)}, ...), condition=%wide.region_5.6_spmd.clone, body=%wide.region_1.5_spmd.clone.sunk | while | flops 543391744 | bytes 27918840 | solution.py:138
  407.9 2.7 dynamic_update_slice.10
  424.9 2.8 dynamic_update_slice.10
  442.0 2.8 dynamic_update_slice.10
  450.7 1.8 select_add_fusion.4
  459.2 2.8 dynamic_update_slice.10
  476.2 2.7 dynamic_update_slice.10
  484.8 1.8 select_add_fusion.4
  493.3 2.8 dynamic_update_slice.10
  502.0 1.8 select_add_fusion.4
  510.4 2.8 dynamic_update_slice.10
  519.1 1.8 select_add_fusion.4
  527.6 2.8 dynamic_update_slice.10
  544.6 2.8 dynamic_update_slice.10
  561.8 2.7 dynamic_update_slice.10
  578.8 2.9 dynamic_update_slice.10
  596.0 2.8 dynamic_update_slice.10
  600.7 2.8 collective-permute-start.4
  603.5 6.7 collective-permute-start.5
  610.2 3.1 collective-permute-done.4
  618.1 1.8 copy.24
  621.1 1.9 collective-permute-start.8
  623.0 7.7 collective-permute-start.9
  632.6 4.0 collective-permute-start.10
  637.9 3.2 collective-permute-done.11
  642.1 236.9 %all-reduce.7.cloned.1.call-done = (f32[2,1024,128]{2,0,1:T(2,128)}, f32[128,128]{1,0:T(8,128)}) async-done(((f32[2,1024,128]{2,0,1:T(2,128)}, f32[128,128]{1,0:T(8,128)}), (f32[2,1024,128]{2,0,1:T(2,128)}, f32[128,128]{1,0:T(8,128)})) %all-reduce.7.cloned.1.call-update) | async-done | bytes 1114128 | tf_op jit(solution)/shard_map/psum | solution.py:144
  882.9 197.0 %while.39 = (s32[]{:T(128)}, f32[3,192,192]{2,1,0:T(8,128)}, f32[2,128,8,128]{3,1,0,2:T(8,128)}, f32[128,128]{1,0:T(8,128)}, s32[12]{0:T(128)S(1)}, /*index=5*/s...) while((s32[]{:T(128)}, f32[3,192,192]{2,1,0:T(8,128)}, ...), condition=%wide.region_13.14_spmd.clone, body=%wide.region_9.13_spmd.clone.sunk | while | flops 543391744 | bytes 27918840 | solution.py:138
  895.7 2.7 dynamic_update_slice.11
  912.0 2.8 dynamic_update_slice.11
  928.4 2.8 dynamic_update_slice.11
  944.9 2.8 dynamic_update_slice.11
  961.3 2.7 dynamic_update_slice.11
  977.7 2.8 dynamic_update_slice.11
  994.2 2.8 dynamic_update_slice.11
  1010.6 2.8 dynamic_update_slice.11
  1027.0 2.8 dynamic_update_slice.11
  1043.4 2.7 dynamic_update_slice.11
  1059.8 2.9 dynamic_update_slice.11
  1076.3 2.8 dynamic_update_slice.11
  1081.0 1.9 collective-permute-start.12
  1082.9 7.5 collective-permute-start.13
  1090.4 3.0 copy.30
  1097.3 3.0 collective-permute-done.15
  1101.9 244.8 %all-reduce.5.cloned.1.call-done = (f32[2,1024,128]{2,0,1:T(2,128)}, f32[128,128]{1,0:T(8,128)}) async-done(((f32[2,1024,128]{2,0,1:T(2,128)}, f32[128,128]{1,0:T(8,128)}), (f32[2,1024,128]{2,0,1:T(2,128)}, f32[128,128]{1,0:T(8,128)})) %all-reduce.5.cloned.1.call-update) | async-done | bytes 1114128 | tf_op jit(solution)/shard_map/psum | solution.py:144
  (689 shorter events, 276.0 us)
Async XLA Ops:
  7.2 384.3 %all-gather.2.cloned.1.call-start = ((), (), s32[]{:S(2)}) async-start(), calls=%async_computation | async-start | bytes 1052672 | tf_op jit(solution)/shard_map/all_gather | solution.py:108
  8.5 870.5 %all-reduce.7.cloned.1.call-start = ((), (), s32[]{:S(2)}) async-start(), calls=%async_computation.2 | async-start | bytes 2228224 | tf_op jit(solution)/shard_map/psum | solution.py:144
  8.6 11.9 collective-permute-start
  12.4 8.9 collective-permute-start.1
  21.4 3.5 collective-permute-start.2
  22.8 5.6 collective-permute-start.3
  407.0 3.6 copy-start.1
  424.1 3.6 copy-start.1
  441.2 3.7 copy-start.1
  458.3 3.6 copy-start.1
  475.4 3.6 copy-start.1
  492.4 3.7 copy-start.1
  509.6 3.6 copy-start.1
  526.7 3.6 copy-start.1
  543.8 3.7 copy-start.1
  560.9 3.5 copy-start.1
  577.9 3.7 copy-start.1
  595.1 3.7 copy-start.1
  599.6 18.5 %copy-start.2 = (f32[2,128,8,128]{3,1,0,2:T(8,128)S(1)}, f32[2,128,8,128]{3,1,0,2:T(8,128)}, u32[]{:S(2)}) copy-start(f32[2,128,8,128]{3,1,0,2:T(8,128)} %get-tuple-element.247) | copy-start | bytes 3145732
  600.7 12.5 collective-permute-start.4
  603.5 10.9 collective-permute-start.5
  615.5 4.5 collective-permute-start.6
  616.8 4.2 collective-permute-start.7
  619.9 260.0 %copy-start.13 = (f32[2,1024,128]{2,0,1:T(2,128)S(1)}, f32[2,1024,128]{2,0,1:T(2,128)}, u32[]{:S(2)}) copy-start(f32[2,1024,128]{2,0,1:T(2,128)} %all-gather.2.cloned.1.call-done) | copy-start | bytes 3145732
  619.9 726.8 %all-reduce.5.cloned.1.call-start = ((), (), s32[]{:S(2)}) async-start(), calls=%async_computation.1 | async-start | bytes 2228224 | tf_op jit(solution)/shard_map/psum | solution.py:144
  621.1 20.1 %copy-start.16 = (f32[2,64,64]{2,1,0:T(8,128)}, f32[2,64,64]{2,1,0:T(8,128)S(1)}, u32[]{:S(2)}) copy-start(f32[2,64,64]{2,1,0:T(8,128)S(1)} %fusion.68) | copy-start | bytes 98308
  621.1 9.9 collective-permute-start.8
  623.0 9.6 collective-permute-start.9
  632.6 5.3 collective-permute-start.10
  636.6 4.5 collective-permute-start.11
  879.9 1.4 copy-start.18
  894.8 3.6 copy-start.4
  911.2 3.6 copy-start.4
  927.6 3.7 copy-start.4
  944.1 3.6 copy-start.4
  960.5 3.6 copy-start.4
  976.8 3.7 copy-start.4
  993.3 3.6 copy-start.4
  1009.7 3.6 copy-start.4
  1026.1 3.7 copy-start.4
  1042.6 3.5 copy-start.4
  1058.9 3.7 copy-start.4
  1075.4 3.7 copy-start.4
  1081.0 12.5 collective-permute-start.12
  1082.9 10.7 collective-permute-start.13
  1094.6 2.6 copy-start.19
  1094.6 2.7 collective-permute-start.14
  1095.9 4.4 collective-permute-start.15
  (148 other events, 135.9 us)
Sparse Core Ops, SparseCore 0:
  10.4 381.0 all-gather.1
  620.0 258.9 all-reduce.6
  1093.6 253.0 all-reduce.4
where the time goes:
time: 1360 us
  waiting for transfers between devices  861 us (63%)
  local copies, waits for them, and re-layouts  158 us (12%)
  other arithmetic  136 us (10%)
  loops' own time  88.1 us (6%)
  starting transfers between devices  51.3 us (4%)
  matrix products  46.9 us (3%)
  between operations  14.2 us (1%)
    psum x2, waiting for transfers between devices, local(): totals, weight_total = lax.psum((grad_rows, weight_probe), ('gy', 'gx'))  482 us
    all_gather x1, waiting for transfers between devices, local(): gathered = lax.all_gather(probe_modes, ('gy', 'gx'), axis=1, tiled=True)  362 us
    another operation x2, loops' own time, local(): lax.scan(visit, initial, (centres[:, 0], centres[:, 1], measured_all))  88.1 us
    dynamic_update_slice x24, local copies, waits for them, and re-layouts, visit(): lax.dynamic_update_slice(grad_obj, before + stacked, (zero_index, row_at,...  66.4 us
    add x48, other arithmetic, visit(): return ((grad_obj, grad_probe + g_probe, weight_probe + w_probe), None)  50.6 us
    while x336, local copies, waits for them, and re-layouts  49.5 us
    dot_general x48, matrix products, transform(): jnp.einsum('crmq,cqdk->drmk', halfway, right_op, preferred_element_type=j...  46.9 us
    sub x24, other arithmetic, position_terms(): shrink = 1.0 - measured / jnp.sqrt(intensity + SOFT_FLOOR)  35.8 us
  transfers between devices with their start and end apart: 19, of which 12 were waited for; matrix products, arithmetic and copies ran while one was open for 1% of the time, Pallas kernels for 0%

commit v1 on v0

--- a/solution.py
+++ b/solution.py
@@ -9,6 +9,9 @@
 SOFT_FLOOR = 0.05
 OBJECT_REG = 1.0
 PROBE_REG = 1.0
+_spread_things = lambda local_array, along_axis, comm_axis: lax.psum(
+    lax.psum(local_array, along_axis), comm_axis
+)
 
 
 def from_behind(block, axis, distance):
@@ -141,7 +144,7 @@
         folded = fold_cols(fold_rows(grad_obj, margin, tile_side), margin, tile_side)
         new_object = current - folded[0:2] / (folded[2] + OBJECT_REG)
         grad_rows = grad_probe.transpose(0, 2, 1, 3).reshape(2, MODES * probe_side, probe_side)
-        totals, weight_total = lax.psum((grad_rows, weight_probe), ("gy", "gx"))
+        totals, weight_total = _spread_things((grad_rows, weight_probe), "gx", "gy")
         whole_probe = probe.transpose(0, 2, 1, 3)
         whole_probe = whole_probe - totals.reshape(2, MODES, probe_side, probe_side) / (
             weight_total[None, None] + PROBE_REG

time: 1360 us -> 1400 us (1.029)
  waiting for transfers between devices: 861 us -> 891 us
    psum x2 -> x4, waiting for transfers between devices: 482 us -> 512 us  [the longest x2 291 us: lax.psum(lax.psum(local_array, along_axis), comm_axis)]
  transfers between devices with their start and end apart: 19 -> 21, of which waited for: 12 -> 13; matrix products, arithmetic and copies ran while one was open for 1% -> 0% of each run, Pallas kernels for 0% -> 0%
where the time goes in v1:
time: 1400 us
  waiting for transfers between devices  891 us (64%)
  local copies, waits for them, and re-layouts  162 us (12%)
  other arithmetic  134 us (10%)
  loops' own time  97.6 us (7%)
  starting transfers between devices  50.6 us (4%)
  matrix products  46.9 us (3%)
  between operations  14.3 us (1%)
    all_gather x1, waiting for transfers between devices, local(): gathered = lax.all_gather(probe_modes, ('gy', 'gx'), axis=1, tiled=True)  362 us
    psum x2, waiting for transfers between devices, lax.psum(lax.psum(local_array, along_axis), comm_axis)  291 us
    psum x2, waiting for transfers between devices, lax.psum(local_array, along_axis)  221 us
    another operation x2, loops' own time, local(): lax.scan(visit, initial, (centres[:, 0], centres[:, 1], measured_all))  97.6 us
    dynamic_update_slice x24, local copies, waits for them, and re-layouts, visit(): lax.dynamic_update_slice(grad_obj, before + stacked, (zero_index, row_at,...  66.4 us
    add x48, other arithmetic, visit(): return ((grad_obj, grad_probe + g_probe, weight_probe + w_probe), None)  50.8 us
    while x336, local copies, waits for them, and re-layouts  49.8 us
    dot_general x48, matrix products, transform(): jnp.einsum('crmq,cqdk->drmk', halfway, right_op, preferred_element_type=j...  46.9 us
  transfers between devices with their start and end apart: 21, of which 13 were waited for; matrix products, arithmetic and copies ran while one was open for 0% of the time, Pallas kernels for 0%

profile of v1, /device:TPU:16, one launch (start us, length us, event | category | flops | bytes accessed | tf_op | source)
XLA Modules:
  0.0 1396.6 jit_solution(8334570063082131564)
XLA Ops:
  8.6 3.8 collective-permute-start
  12.4 5.6 collective-permute-start.1
  24.8 3.6 collective-permute-done.3
  29.3 362.2 %all-gather.2.cloned.1.call-done = f32[2,1024,128]{2,0,1:T(2,128)} async-done(((f32[2,4,128]{2,0,1:T(2,128)}), f32[2,1024,128]{2,0,1:T(2,128)}) %all-gather.2.cloned.1.call-update) | async-done | bytes 1048592 | tf_op jit(solution)/shard_map/all_gather | solution.py:111
  394.4 205.6 %while.38 = (s32[]{:T(128)}, f32[3,192,192]{2,1,0:T(8,128)}, f32[2,128,8,128]{3,1,0,2:T(8,128)}, f32[128,128]{1,0:T(8,128)}, s32[12]{0:T(128)S(1)}, /*index=5*/s...) while((s32[]{:T(128)}, f32[3,192,192]{2,1,0:T(8,128)}, ...), condition=%wide.region_5.6_spmd.clone, body=%wide.region_1.5_spmd.clone.sunk | while | flops 543391744 | bytes 27918840 | solution.py:141
  407.9 2.7 dynamic_update_slice.10
  425.0 2.8 dynamic_update_slice.10
  442.1 2.8 dynamic_update_slice.10
  459.3 2.8 dynamic_update_slice.10
  476.4 2.7 dynamic_update_slice.10
  493.5 2.8 dynamic_update_slice.10
  510.7 2.8 dynamic_update_slice.10
  527.8 2.8 dynamic_update_slice.10
  544.9 2.8 dynamic_update_slice.10
  562.1 2.7 dynamic_update_slice.10
  579.1 2.9 dynamic_update_slice.10
  596.4 2.8 dynamic_update_slice.10
  600.0 3.0 copy.24
  604.1 2.8 collective-permute-start.4
  606.9 6.7 collective-permute-start.5
  613.6 3.6 collective-permute-done.4
  618.4 107.5 %all-reduce.15.cloned.1.call-done = (f32[2,1024,128]{2,0,1:T(2,128)}, f32[128,128]{1,0:T(8,128)}) async-done(((f32[2,1024,128]{2,0,1:T(2,128)}, f32[128,128]{1,0:T(8,128)}), (f32[2,1024,128]{2,0,1:T(2,128)}, f32[128,128]{1,0:T(8,128)})) %all-reduce.15.cloned.1.call-update) | async-done | bytes 1114128 | tf_op jit(solution)/shard_map/psum | solution.py:13
  728.8 1.9 collective-permute-done.7
  730.8 3.5 collective-permute-start.8
  734.3 6.0 collective-permute-start.9
  742.2 3.2 collective-permute-start.10
  746.7 2.6 collective-permute-done.11
  750.2 136.7 %all-reduce.11.cloned.1.call-done = (f32[2,1024,128]{2,0,1:T(2,128)}, f32[128,128]{1,0:T(8,128)}) async-done(((f32[2,1024,128]{2,0,1:T(2,128)}, f32[128,128]{1,0:T(8,128)}), (f32[2,1024,128]{2,0,1:T(2,128)}, f32[128,128]{1,0:T(8,128)})) %all-reduce.11.cloned.1.call-update) | async-done | bytes 1114128 | tf_op jit(solution)/shard_map/psum | solution.py:12
  890.8 209.3 %while.39 = (s32[]{:T(128)}, f32[3,192,192]{2,1,0:T(8,128)}, f32[2,128,8,128]{3,1,0,2:T(8,128)}, f32[128,128]{1,0:T(8,128)}, s32[12]{0:T(128)S(1)}, /*index=5*/s...) while((s32[]{:T(128)}, f32[3,192,192]{2,1,0:T(8,128)}, ...), condition=%wide.region_15.16_spmd.clone, body=%wide.region_11.15_spmd.clone.sunk | while | flops 543391744 | bytes 27918840 | solution.py:141
  904.6 2.7 dynamic_update_slice.11
  913.5 1.8 select_add_fusion.5
  921.9 2.8 dynamic_update_slice.11
  939.4 2.8 dynamic_update_slice.11
  956.9 2.8 dynamic_update_slice.11
  974.3 2.7 dynamic_update_slice.11
  991.7 2.8 dynamic_update_slice.11
  1009.2 2.8 dynamic_update_slice.11
  1026.6 2.8 dynamic_update_slice.11
  1044.0 2.8 dynamic_update_slice.11
  1061.5 2.7 dynamic_update_slice.11
  1078.9 2.9 dynamic_update_slice.11
  1096.4 2.8 dynamic_update_slice.11
  1100.0 3.0 copy.30
  1104.2 2.4 collective-permute-start.12
  1106.5 7.1 collective-permute-start.13
  1113.6 113.9 %all-reduce.13.cloned.1.call-done = (f32[2,1024,128]{2,0,1:T(2,128)}, f32[128,128]{1,0:T(8,128)}) async-done(((f32[2,1024,128]{2,0,1:T(2,128)}, f32[128,128]{1,0:T(8,128)}), (f32[2,1024,128]{2,0,1:T(2,128)}, f32[128,128]{1,0:T(8,128)})) %all-reduce.13.cloned.1.call-update) | async-done | bytes 1114128 | tf_op jit(solution)/shard_map/psum | solution.py:13
  1230.4 1.8 collective-permute-done.15
  1233.8 154.1 %all-reduce.9.cloned.1.call-done = (f32[2,1024,128]{2,0,1:T(2,128)}, f32[128,128]{1,0:T(8,128)}) async-done(((f32[2,1024,128]{2,0,1:T(2,128)}, f32[128,128]{1,0:T(8,128)}), (f32[2,1024,128]{2,0,1:T(2,128)}, f32[128,128]{1,0:T(8,128)})) %all-reduce.9.cloned.1.call-update) | async-done | bytes 1114128 | tf_op jit(solution)/shard_map/psum | solution.py:12
  (697 shorter events, 281.5 us)
Async XLA Ops:
  7.2 384.3 %all-gather.2.cloned.1.call-start = ((), (), s32[]{:S(2)}) async-start(), calls=%async_computation | async-start | bytes 1052672 | tf_op jit(solution)/shard_map/all_gather | solution.py:111
  8.5 717.4 %all-reduce.15.cloned.1.call-start = ((), (), s32[]{:S(2)}) async-start(), calls=%async_computation.4 | async-start | bytes 2228224 | tf_op jit(solution)/shard_map/psum | solution.py:13
  8.6 11.9 collective-permute-start
  12.4 8.9 collective-permute-start.1
  21.4 3.5 collective-permute-start.2
  22.8 5.6 collective-permute-start.3
  407.1 3.6 copy-start.1
  424.1 3.6 copy-start.1
  441.3 3.7 copy-start.1
  458.4 3.6 copy-start.1
  475.6 3.6 copy-start.1
  492.6 3.7 copy-start.1
  509.8 3.6 copy-start.1
  527.0 3.6 copy-start.1
  544.1 3.7 copy-start.1
  561.3 3.5 copy-start.1
  578.3 3.7 copy-start.1
  595.5 3.7 copy-start.1
  603.1 283.8 %all-reduce.11.cloned.1.call-start = ((), (), s32[]{:S(2)}) async-start(), calls=%async_computation.2 | async-start | bytes 2228224 | tf_op jit(solution)/shard_map/psum | solution.py:12
  604.1 13.1 collective-permute-start.4
  606.9 11.4 collective-permute-start.5
  725.9 501.7 %all-reduce.13.cloned.1.call-start = ((), (), s32[]{:S(2)}) async-start(), calls=%async_computation.3 | async-start | bytes 2228224 | tf_op jit(solution)/shard_map/psum | solution.py:13
  726.0 4.8 copy-start.22
  726.0 2.7 collective-permute-start.6
  727.3 160.5 %copy-start.14 = (f32[2,1024,128]{2,0,1:T(2,128)S(1)}, f32[2,1024,128]{2,0,1:T(2,128)}, u32[]{:S(2)}) copy-start(f32[2,1024,128]{2,0,1:T(2,128)} %all-gather.2.cloned.1.call-done) | copy-start | bytes 3145732
  727.3 3.3 collective-permute-start.7
  730.8 18.5 %copy-start.17 = (f32[2,64,64]{2,1,0:T(8,128)}, f32[2,64,64]{2,1,0:T(8,128)S(1)}, u32[]{:S(2)}) copy-start(f32[2,64,64]{2,1,0:T(8,128)S(1)} %fusion.68) | copy-start | bytes 98308
  730.8 9.8 collective-permute-start.8
  734.3 7.9 collective-permute-start.9
  742.2 4.5 collective-permute-start.10
  745.4 3.9 collective-permute-start.11
  903.7 3.6 copy-start.3
  921.1 3.6 copy-start.3
  938.5 3.7 copy-start.3
  956.0 3.6 copy-start.3
  973.4 3.6 copy-start.3
  990.8 3.7 copy-start.3
  1008.3 3.6 copy-start.3
  1025.8 3.6 copy-start.3
  1043.2 3.7 copy-start.3
  1060.7 3.5 copy-start.3
  1078.0 3.7 copy-start.3
  1095.6 3.7 copy-start.3
  1103.1 284.8 %all-reduce.9.cloned.1.call-start = ((), (), s32[]{:S(2)}) async-start(), calls=%async_computation.1 | async-start | bytes 2228224 | tf_op jit(solution)/shard_map/psum | solution.py:12
  1104.2 123.4 %collective-permute-start.12 = (f32[3,64,192]{2,1,0:T(8,128)S(1)}, f32[3,64,192]{2,1,0:T(8,128)S(1)}, u32[]{:S(2)}, u32[]{:S(2)}) collective-permute-start(f32[3,64,192]{2,1,0:T(8,128)S(1)} %get-tuple-element.486), channel_id=1, source_target_pairs={{0,1},{1,2},{2,3},{3,4},{4,5},{5,6},{6,7},{7,8},{8,9},{9,10},{10,1... | collective-permute-start | bytes 442376 | tf_op jit(solution)/shard_map/ppermute | solution.py:20
  1106.5 121.1 %collective-permute-start.13 = (f32[3,64,192]{2,1,0:T(8,128)S(1)}, f32[3,64,192]{2,1,0:T(8,128)S(1)}, u32[]{:S(2)}, u32[]{:S(2)}) collective-permute-start(f32[3,64,192]{2,1,0:T(8,128)S(1)} %get-tuple-element.487), channel_id=1, source_target_pairs={{1,0},{2,1},{3,2},{4,3},{5,4},{6,5},{7,6},{8,7},{9,8},{10,9},{11,1... | collective-permute-start | bytes 442376 | tf_op jit(solution)/shard_map/ppermute | solution.py:20
  1227.7 2.7 collective-permute-start.14
  1229.0 3.2 collective-permute-start.15
  (151 other events, 141.3 us)
Sparse Core Ops, SparseCore 0:
  10.4 381.0 all-gather.1
  603.2 122.6 all-reduce.14
  728.6 158.2 all-reduce.10
  1103.2 124.3 all-reduce.12
  1230.2 157.6 all-reduce.8
